TPU v7x, 512 devices: a whole 4x4x16 slice. The times are simulated.
512 devices in a mesh: spec: 16 (over y, x), tile: 32 (over z, core).
Axes of the slice: x: 4, y: 4, z: 16, core: 2. Of those that a mesh axis runs over, the one named last changes fastest.
Arguments:
- action: bfloat16 [512, 3072, 256], P('tile', 'spec'), may hold values from 0.099609375 to 2
- east_current: float32 [512, 256], P('tile'), may hold values from -0.4 to 0.4
- north_current: float32 [512, 256], P('tile'), may hold values from -0.4 to 0.4
- sea_mask: int32 [512, 256], P('tile'), may hold values from 0 to 1, as said below
- pattern: int32 [48, 24], replicated, may hold values from 0 to 47, as said below
- table: bfloat16 [48, 64, 64], replicated, may hold values from -0.15625 to 0.15625
Outputs:
- updated: bfloat16 [512, 3072, 256], P('tile', 'spec')
Inputs may be any that keep to these rules, and one draw needn't show every extreme that they name: `sea_mask`: each tile of 16 latitude rows (all 256 longitudes) holds at most 2048 sea points, and in every draw some tile holds exactly 2048. `pattern`: each row names 24 different direction blocks.
All inputs are finite; a program needn't handle non-finite values.
Results may differ from a plain program's by a relative error of at most 0.0043.
Values may be sent and summed in bfloat16 or wider, within the bound.
A program may use at most 64 MiB of HBM per device.

v0:
```python
import jax
import jax.numpy as jnp
from jax import lax
from jax.sharding import PartitionSpec as P

NF = 64
ND = 48
SUB = 2
courant_scale = 0.45


def extended(cells, sides, width):
    for axis, dim in sides:
        count = lax.axis_size(axis)
        ends = count - 1
        head = lax.slice_in_dim(cells, 0, width, axis=dim)
        tail = lax.slice_in_dim(cells, cells.shape[dim] - width, cells.shape[dim], axis=dim)
        cells = jnp.concatenate(
            [
                lax.ppermute(tail, axis, [(i, (i + 1) % count) for i in range(ends)]),
                cells,
                lax.ppermute(head, axis, [((i + 1) % count, i) for i in range(ends)]),
            ],
            axis=dim,
        )
    return cells


def upwind(padded, courant_east, courant_north):
    center = padded[1:-1]
    south_row = padded[:-2]
    north_row = padded[2:]
    zero_column = jnp.zeros_like(center[:, :, :1])
    west_cell = jnp.concatenate([zero_column, center[:, :, :-1]], axis=2)
    east_cell = jnp.concatenate([center[:, :, 1:], zero_column], axis=2)
    return (
        center
        - jnp.maximum(courant_east, 0.0) * (center - west_cell)
        - jnp.minimum(courant_east, 0.0) * (east_cell - center)
        - jnp.maximum(courant_north, 0.0) * (center - south_row)
        - jnp.minimum(courant_north, 0.0) * (north_row - center)
    )


def source_update(cell_action, cell_mask, pattern, table):
    row_count = cell_action.shape[0]
    lane_count = cell_action.shape[2]
    group_size = 8
    offsets = (pattern - jnp.arange(ND, dtype=jnp.int32)[:, None]) % ND
    directions = jnp.arange(ND, dtype=jnp.int32)

    def advance_group(unused_state, group_rows):
        selector = (pattern[group_rows][:, :, None] == directions[None, None, :]).astype(
            jnp.float32
        )
        weights = table[offsets[group_rows]].astype(jnp.float32)
        assembled = jnp.einsum("rjc,rjab->racb", selector, weights)
        assembled = assembled.astype(jnp.bfloat16).reshape(group_size * NF, ND * NF)
        coupled = jnp.einsum(
            "ak,rkl->ral", assembled, cell_action, preferred_element_type=jnp.float32
        )
        return (unused_state, coupled)

    group_index = directions.reshape(ND // group_size, group_size)
    unused_state, coupled = lax.scan(advance_group, jnp.zeros((), jnp.float32), group_index)
    coupled = jnp.transpose(coupled, (1, 0, 2, 3)).reshape(row_count, ND * NF, lane_count)
    own_action = cell_action.astype(jnp.float32)
    sea_part = cell_mask.astype(jnp.float32)[:, None, :]
    result = own_action + sea_part * own_action * coupled
    return result.astype(jnp.bfloat16)


def local(action, east_current, north_current, sea_mask, pattern, table):
    tile_rows = action.shape[0]
    comp_count = action.shape[1]
    spec_count = lax.axis_size("spec")
    spec_index = lax.axis_index("spec")
    components = spec_index * comp_count + jnp.arange(comp_count, dtype=jnp.int32)
    direction = (components // NF).astype(jnp.float32)
    frequency = (components % NF).astype(jnp.float32)
    speed = jnp.exp(-2.0 * frequency / (NF - 1))
    theta = 2.0 * jnp.pi * direction / ND
    courant_east = courant_scale * (
        (speed * jnp.cos(theta))[None, :, None] + east_current[:, None, :]
    )
    courant_north = courant_scale * (
        (speed * jnp.sin(theta))[None, :, None] + north_current[:, None, :]
    )
    field = action.astype(jnp.float32)
    for substep in range(SUB):
        padded = extended(field, (("tile", 0),), 1)
        field = upwind(padded, courant_east, courant_north)
    moved = field.astype(jnp.bfloat16)
    share_rows = tile_rows // spec_count
    incoming = lax.all_to_all(moved, "spec", split_axis=0, concat_axis=1, tiled=True)
    own_mask = lax.dynamic_slice_in_dim(sea_mask, spec_index * share_rows, share_rows, 0)
    renewed = source_update(incoming, own_mask, pattern, table)
    result = lax.all_to_all(renewed, "spec", split_axis=1, concat_axis=0, tiled=True)
    return result


def solution(mesh):
    return jax.shard_map(
        local,
        mesh=mesh,
        in_specs=(
            P("tile", "spec", None),
            P("tile", None),
            P("tile", None),
            P("tile", None),
            P(),
            P(),
        ),
        out_specs=P("tile", "spec", None),
        check_vma=False,
    )
```

profile of v0, /device:TPU:320, one launch (start us, length us, event | category | flops | bytes accessed | tf_op | source)
XLA Modules:
  0.0 262.7 jit_solution(9454348573724922030)
XLA Ops:
  2.9 3.8 %collective-permute-start.1 = (f32[1,192,256]{2,1,0:T(8,128)S(1)}, f32[1,192,256]{2,1,0:T(8,128)S(1)}, u32[]{:S(2)}, u32[]{:S(2)}) collective-permute-start(f32[1,192,256]{2,1,0:T(8,128)S(1)} %get-tuple-element.106), channel_id=1, source_target_pairs={{1,0},{2,1},{3,2},{4,3},{5,4},{6,5},{7,6},{8,7},{9,8},{10,9},{11,1... | collective-permute-start | bytes 589832 | tf_op jit(solution)/shard_map/ppermute | solution.py:22
  6.7 5.5 %fusion.41 = (f32[16,192,255]{2,1,0:T(8,128)}, f32[16,192,255]{2,1,0:T(8,128)}) fusion(bf16[16,192,256]{2,1,0:T(8,128)(2,1)} %param.8), kind=kLoop, calls=%fused_computation.71 | loop fusion | bytes 12533760 | tf_op jit(solution)/shard_map/slice | solution.py:34
  14.3 5.8 %fusion.18 = f32[16,192,256]{2,1,0:T(8,128)S(1)} fusion(bf16[16,192,256]{2,1,0:T(8,128)(2,1)S(1)} %copy-done, f32[1,192,256]{2,1,0:T(8,128)S(1)} %collective-permute-done.1, f32[16,192,256]{2,1,0:T(8,128)} %convert_element_type.59, f32[1,192,256]{2,1,0:T(8,128)S(1)} %collective-permute-done, f32[16,192,255]{2,1,0:T(8,128)} %get-tuple-element.104, ...), kind=kLoop, calls=%fused_computation.28 | loop fusion | flops 18087936 | bytes 14558720 | tf_op jit(solution)/shard_map/sub | solution.py:37
  28.9 3.9 %fusion.27 = bf16[16,192,256]{2,1,0:T(8,128)(2,1)} fusion(f32[16,192,256]{2,1,0:T(8,128)S(1)} %fusion.18, f32[1,192,256]{2,1,0:T(8,128)S(1)} %collective-permute-done.3, f32[1,192,256]{2,1,0:T(8,128)S(1)} %collective-permute-done.2, f32[16,192,255]{2,1,0:T(8,128)S(1)} %get-tuple-element.100, f32[16,192,255]{2,1,0:T(8,128)S(1)} %get-tuple-element.99, ...), kind=kLoop, calls=%fused_computation.38 | loop fusion | flops 18087936 | bytes 11412992 | tf_op jit(solution)/shard_map/convert_element_type | solution.py:93
  32.8 7.2 %all-to-all-start = ((bf16[16,192,256]{2,1,0:T(8,128)(2,1)}), bf16[16,192,256]{2,1,0:T(8,128)(2,1)}, u32[]{:S(2)}, u32[]{:S(2)}) async-start(bf16[16,192,256]{2,1,0:T(8,128)(2,1)} %fusion.27), calls=%async_computation | async-start | bytes 3145728 | tf_op jit(solution)/shard_map/all_to_all | solution.py:95
  40.9 27.2 %all-to-all-done = bf16[16,192,256]{2,1,0:T(8,128)(2,1)} async-done(((bf16[16,192,256]{2,1,0:T(8,128)(2,1)}), bf16[16,192,256]{2,1,0:T(8,128)(2,1)}, u32[]{:S(2)}, u32[]{:S(2)}) %all-to-all-start) | async-done | bytes 1572896 | tf_op jit(solution)/shard_map/all_to_all | solution.py:95
  68.0 117.2 %while.11 = (s32[]{:T(128)}, f32[6,1,512,256]{3,2,1,0:T(8,128)}, s32[6,8]{1,0:T(8,128)S(1)}, s32[48,24]{1,0:T(8,128)S(1)}, bf16[48,64,64]{2,1,0:T(8,128)(2,1)}, ...) while((s32[]{:T(128)}, f32[6,1,512,256]{3,2,1,0:T(8,128)}, ...), condition=%wide.region_1.2_spmd.clone, body=%wide.region_0.1_spmd.clone.sunk | while | flops 882388544 | bytes 19416056 | solution.py:65
  71.6 5.3 %convert_bitcast_fusion.2 = bf16[8,64,48,64]{3,2,1,0:T(8,128)(2,1)} fusion(bf16[8,24,64,64]{3,2,1,0:T(8,128)(2,1)S(1)} %bitcast.64, s32[8,24]{1,0:T(8,128)S(1)} %gather_fusion.2), kind=kOutput, calls=%fused_computation.4.clone.1 | convolution fusion | flops 77079552 | bytes 4719360 | tf_op jit(solution)/shard_map/while/body/eval_jaxpr/rjc,rjab->racb/dot_general | solution.py:57
  76.8 7.5 %reshape.229 = bf16[512,3072]{1,0:T(8,128)(2,1)S(1)} reshape(bf16[8,64,48,64]{3,2,1,0:T(8,128)(2,1)} %convert_bitcast_fusion.2) | data formatting | bytes 6291456 | tf_op jit(solution)/shard_map/while/body/eval_jaxpr/reshape | solution.py:58
  91.1 5.3 %convert_bitcast_fusion.2 = bf16[8,64,48,64]{3,2,1,0:T(8,128)(2,1)} fusion(bf16[8,24,64,64]{3,2,1,0:T(8,128)(2,1)S(1)} %bitcast.64, s32[8,24]{1,0:T(8,128)S(1)} %gather_fusion.2), kind=kOutput, calls=%fused_computation.4.clone.1 | convolution fusion | flops 77079552 | bytes 4719360 | tf_op jit(solution)/shard_map/while/body/eval_jaxpr/rjc,rjab->racb/dot_general | solution.py:57
  96.4 7.5 %reshape.229 = bf16[512,3072]{1,0:T(8,128)(2,1)S(1)} reshape(bf16[8,64,48,64]{3,2,1,0:T(8,128)(2,1)} %convert_bitcast_fusion.2) | data formatting | bytes 6291456 | tf_op jit(solution)/shard_map/while/body/eval_jaxpr/reshape | solution.py:58
  110.6 5.3 %convert_bitcast_fusion.2 = bf16[8,64,48,64]{3,2,1,0:T(8,128)(2,1)} fusion(bf16[8,24,64,64]{3,2,1,0:T(8,128)(2,1)S(1)} %bitcast.64, s32[8,24]{1,0:T(8,128)S(1)} %gather_fusion.2), kind=kOutput, calls=%fused_computation.4.clone.1 | convolution fusion | flops 77079552 | bytes 4719360 | tf_op jit(solution)/shard_map/while/body/eval_jaxpr/rjc,rjab->racb/dot_general | solution.py:57
  115.9 7.5 %reshape.229 = bf16[512,3072]{1,0:T(8,128)(2,1)S(1)} reshape(bf16[8,64,48,64]{3,2,1,0:T(8,128)(2,1)} %convert_bitcast_fusion.2) | data formatting | bytes 6291456 | tf_op jit(solution)/shard_map/while/body/eval_jaxpr/reshape | solution.py:58
  130.1 5.3 %convert_bitcast_fusion.2 = bf16[8,64,48,64]{3,2,1,0:T(8,128)(2,1)} fusion(bf16[8,24,64,64]{3,2,1,0:T(8,128)(2,1)S(1)} %bitcast.64, s32[8,24]{1,0:T(8,128)S(1)} %gather_fusion.2), kind=kOutput, calls=%fused_computation.4.clone.1 | convolution fusion | flops 77079552 | bytes 4719360 | tf_op jit(solution)/shard_map/while/body/eval_jaxpr/rjc,rjab->racb/dot_general | solution.py:57
  135.4 7.5 %reshape.229 = bf16[512,3072]{1,0:T(8,128)(2,1)S(1)} reshape(bf16[8,64,48,64]{3,2,1,0:T(8,128)(2,1)} %convert_bitcast_fusion.2) | data formatting | bytes 6291456 | tf_op jit(solution)/shard_map/while/body/eval_jaxpr/reshape | solution.py:58
  149.6 5.3 %convert_bitcast_fusion.2 = bf16[8,64,48,64]{3,2,1,0:T(8,128)(2,1)} fusion(bf16[8,24,64,64]{3,2,1,0:T(8,128)(2,1)S(1)} %bitcast.64, s32[8,24]{1,0:T(8,128)S(1)} %gather_fusion.2), kind=kOutput, calls=%fused_computation.4.clone.1 | convolution fusion | flops 77079552 | bytes 4719360 | tf_op jit(solution)/shard_map/while/body/eval_jaxpr/rjc,rjab->racb/dot_general | solution.py:57
  154.9 7.5 %reshape.229 = bf16[512,3072]{1,0:T(8,128)(2,1)S(1)} reshape(bf16[8,64,48,64]{3,2,1,0:T(8,128)(2,1)} %convert_bitcast_fusion.2) | data formatting | bytes 6291456 | tf_op jit(solution)/shard_map/while/body/eval_jaxpr/reshape | solution.py:58
  169.2 5.3 %convert_bitcast_fusion.2 = bf16[8,64,48,64]{3,2,1,0:T(8,128)(2,1)} fusion(bf16[8,24,64,64]{3,2,1,0:T(8,128)(2,1)S(1)} %bitcast.64, s32[8,24]{1,0:T(8,128)S(1)} %gather_fusion.2), kind=kOutput, calls=%fused_computation.4.clone.1 | convolution fusion | flops 77079552 | bytes 4719360 | tf_op jit(solution)/shard_map/while/body/eval_jaxpr/rjc,rjab->racb/dot_general | solution.py:57
  174.5 7.5 %reshape.229 = bf16[512,3072]{1,0:T(8,128)(2,1)S(1)} reshape(bf16[8,64,48,64]{3,2,1,0:T(8,128)(2,1)} %convert_bitcast_fusion.2) | data formatting | bytes 6291456 | tf_op jit(solution)/shard_map/while/body/eval_jaxpr/reshape | solution.py:58
  188.0 17.5 %copy.23 = bf16[1,3072,256]{2,0,1:T(2,128)(2,1)S(1)} copy(bf16[1,3072,256]{2,1,0:T(8,128)(2,1)S(1)} %fusion.23) | data formatting | bytes 3145728 | tf_op jit(solution)/shard_map/convert_element_type | solution.py:70
  206.1 16.6 %reduce = bf16[3072,256]{1,0:T(8,128)(2,1)} reduce(bf16[3072,1,256]{2,1,0:T(2,128)(2,1)S(1)} %bitcast.65, bf16[]{:T(256)} %broadcast.244), dimensions={1}, to_apply=%bitcast.44.reduce_sub_computation | reduce | bytes 3145730
  222.7 3.7 %reshape.212 = bf16[16,2,24576]{2,1,0:T(2,128)(2,1)S(1)} reshape(bf16[3072,256]{1,0:T(8,128)(2,1)} %reduce) | data formatting | bytes 3145728
  226.5 26.7 %all_to_all.24 = bf16[16,2,24576]{2,1,0:T(2,128)(2,1)} all-to-all(bf16[16,2,24576]{2,1,0:T(2,128)(2,1)S(1)} %reshape.212), channel_id=1, replica_groups=mesh['spec'=16,'tile'=32] {'spec'}, dimensions={0} | all-to-all | bytes 3145728 | tf_op jit(solution)/shard_map/all_to_all | solution.py:98
  253.2 8.1 %reshape.213 = bf16[3072,1,256]{2,1,0:T(2,128)(2,1)S(1)} reshape(bf16[16,2,24576]{2,1,0:T(2,128)(2,1)} %all_to_all.24) | data formatting | bytes 3145728
  (82 shorter events, 59.5 us)
Async XLA Ops:
  1.0 13.2 %collective-permute-start = (f32[1,192,256]{2,1,0:T(8,128)S(1)}, f32[1,192,256]{2,1,0:T(8,128)S(1)}, u32[]{:S(2)}, u32[]{:S(2)}) collective-permute-start(f32[1,192,256]{2,1,0:T(8,128)S(1)} %get-tuple-element.105), channel_id=1, source_target_pairs={{0,1},{1,2},{2,3},{3,4},{4,5},{5,6},{6,7},{7,8},{8,9},{9,10},{10,1... | collective-permute-start | bytes 589832 | tf_op jit(solution)/shard_map/ppermute | solution.py:20
  2.9 9.3 %copy-start = (bf16[16,192,256]{2,1,0:T(8,128)(2,1)S(1)}, bf16[16,192,256]{2,1,0:T(8,128)(2,1)}, u32[]{:S(2)}) copy-start(bf16[16,192,256]{2,1,0:T(8,128)(2,1)} %param.8) | copy-start | bytes 4718596
  2.9 11.3 %collective-permute-start.1 = (f32[1,192,256]{2,1,0:T(8,128)S(1)}, f32[1,192,256]{2,1,0:T(8,128)S(1)}, u32[]{:S(2)}, u32[]{:S(2)}) collective-permute-start(f32[1,192,256]{2,1,0:T(8,128)S(1)} %get-tuple-element.106), channel_id=1, source_target_pairs={{1,0},{2,1},{3,2},{4,3},{5,4},{6,5},{7,6},{8,7},{9,8},{10,9},{11,1... | collective-permute-start | bytes 589832 | tf_op jit(solution)/shard_map/ppermute | solution.py:22
  12.2 2.1 copy-start.1
  12.2 2.1 copy-start.2
  20.1 7.0 %collective-permute-start.2 = (f32[1,192,256]{2,1,0:T(8,128)S(1)}, f32[1,192,256]{2,1,0:T(8,128)S(1)}, u32[]{:S(2)}, u32[]{:S(2)}) collective-permute-start(f32[1,192,256]{2,1,0:T(8,128)S(1)} %get-tuple-element.101), channel_id=1, source_target_pairs={{0,1},{1,2},{2,3},{3,4},{4,5},{5,6},{6,7},{7,8},{8,9},{9,10},{10,1... | collective-permute-start | bytes 589832 | tf_op jit(solution)/shard_map/ppermute | solution.py:20
  22.1 6.8 %collective-permute-start.3 = (f32[1,192,256]{2,1,0:T(8,128)S(1)}, f32[1,192,256]{2,1,0:T(8,128)S(1)}, u32[]{:S(2)}, u32[]{:S(2)}) collective-permute-start(f32[1,192,256]{2,1,0:T(8,128)S(1)} %get-tuple-element.102), channel_id=1, source_target_pairs={{1,0},{2,1},{3,2},{4,3},{5,4},{6,5},{7,6},{8,7},{9,8},{10,9},{11,1... | collective-permute-start | bytes 589832 | tf_op jit(solution)/shard_map/ppermute | solution.py:22
  32.8 7.2 %copy-start.3 = (s32[48,24]{0,1:T(8,128)S(1)}, s32[48,24]{0,1:T(8,128)}, u32[]{:S(2)}) copy-start(s32[48,24]{0,1:T(8,128)} %param.12) | copy-start | bytes 13828
  32.8 35.2 %all-to-all-start = ((bf16[16,192,256]{2,1,0:T(8,128)(2,1)}), bf16[16,192,256]{2,1,0:T(8,128)(2,1)}, u32[]{:S(2)}, u32[]{:S(2)}) async-start(bf16[16,192,256]{2,1,0:T(8,128)(2,1)} %fusion.27), calls=%async_computation | async-start | bytes 3145728 | tf_op jit(solution)/shard_map/all_to_all | solution.py:95
where the time goes:
time: 265 us; the launch traced here: 263 us
  local copies, waits for them, and re-layouts  105 us (40%)
  matrix products  50.9 us (19%)
  other arithmetic  32.1 us (12%)
  waiting for transfers between devices  29.2 us (11%)
  blocking collectives  26.7 us (10%)
  starting transfers between devices  18.5 us (7%)
    reshape x6, local copies, waits for them, and re-layouts, advance_group(): assembled = assembled.astype(jnp.bfloat16).reshape(group_size * NF, ND * NF)  45 us
    dot_general x6, matrix products, advance_group(): assembled = jnp.einsum('rjc,rjab->racb', selector, weights)  31.6 us
    all_to_all x1, waiting for transfers between devices, local(): lax.all_to_all(moved, 'spec', split_axis=0, concat_axis=1, tiled=True)  27.2 us
    all_to_all x1, blocking collectives, local(): lax.all_to_all(renewed, 'spec', split_axis=1, concat_axis=0, tiled=True)  26.7 us
    dot_general x6, matrix products, advance_group(): jnp.einsum('ak,rkl->ral', assembled, cell_action, preferred_element_type=...  19.2 us
    convert_element_type x1, local copies, waits for them, and re-layouts, source_update(): return result.astype(jnp.bfloat16)  17.5 us
    gather x12, local copies, waits for them, and re-layouts, advance_group(): weights = table[offsets[group_rows]].astype(jnp.float32)  17.1 us
    unnamed x1, other arithmetic  16.6 us
  transfers between devices with their start and end apart: 5, of which 3 were waited for; matrix products, arithmetic and copies ran while one was open for 4% of the time, Pallas kernels for 0%

commit v1 on v0

--- a/solution.py
+++ b/solution.py
@@ -95,7 +95,10 @@
     incoming = lax.all_to_all(moved, "spec", split_axis=0, concat_axis=1, tiled=True)
     own_mask = lax.dynamic_slice_in_dim(sea_mask, spec_index * share_rows, share_rows, 0)
     renewed = source_update(incoming, own_mask, pattern, table)
-    result = lax.all_to_all(renewed, "spec", split_axis=1, concat_axis=0, tiled=True)
+    result = jnp.concatenate(
+        lax.all_to_all(jnp.stack(jnp.split(renewed, lax.axis_size("spec"), axis=1)), "spec", 0, 0),
+        0,
+    )
     return result
 
 

time: 265 us -> 217 us (0.82)
  the two profiles are of different devices: /device:TPU:320 before, /device:TPU:448 now
where the time goes in v1:
time: 217 us; the launch traced here: 216 us
  local copies, waits for them, and re-layouts  75 us (35%)
  matrix products  50.9 us (23%)
  waiting for transfers between devices  29.2 us (13%)
  blocking collectives  26 us (12%)
  starting transfers between devices  18.5 us (9%)
  other arithmetic  15.5 us (7%)
    reshape x6, local copies, waits for them, and re-layouts, advance_group(): assembled = assembled.astype(jnp.bfloat16).reshape(group_size * NF, ND * NF)  45 us
    dot_general x6, matrix products, advance_group(): assembled = jnp.einsum('rjc,rjab->racb', selector, weights)  31.7 us
    all_to_all x1, waiting for transfers between devices, local(): lax.all_to_all(moved, 'spec', split_axis=0, concat_axis=1, tiled=True)  27.2 us
    all_to_all x1, blocking collectives, local(): lax.all_to_all(jnp.stack(jnp.split(renewed, lax.axis_size('spec'), axis=1...  26 us
    dot_general x6, matrix products, advance_group(): jnp.einsum('ak,rkl->ral', assembled, cell_action, preferred_element_type=...  19.2 us
    gather x12, local copies, waits for them, and re-layouts, advance_group(): weights = table[offsets[group_rows]].astype(jnp.float32)  17.1 us
    ppermute x2, starting transfers between devices, extended(): lax.ppermute(head, axis, [((i + 1) % count, i) for i in range(ends)])  7.42 us
    all_to_all x1, starting transfers between devices, local(): lax.all_to_all(moved, 'spec', split_axis=0, concat_axis=1, tiled=True)  7.21 us
  transfers between devices with their start and end apart: 5, of which 3 were waited for; matrix products, arithmetic and copies ran while one was open for 4% of the time, Pallas kernels for 0%

profile of v1, /device:TPU:448, one launch (start us, length us, event | category | flops | bytes accessed | tf_op | source)
XLA Modules:
  0.0 215.5 jit_solution(1481208219118710369)
XLA Ops:
  2.9 3.8 %collective-permute-start.1 = (f32[1,192,256]{2,1,0:T(8,128)S(1)}, f32[1,192,256]{2,1,0:T(8,128)S(1)}, u32[]{:S(2)}, u32[]{:S(2)}) collective-permute-start(f32[1,192,256]{2,1,0:T(8,128)S(1)} %get-tuple-element.99), channel_id=1, source_target_pairs={{1,0},{2,1},{3,2},{4,3},{5,4},{6,5},{7,6},{8,7},{9,8},{10,9},{11,1... | collective-permute-start | bytes 589832 | tf_op jit(solution)/shard_map/ppermute | solution.py:22
  6.7 5.5 %fusion.57 = (f32[16,192,255]{2,1,0:T(8,128)}, f32[16,192,255]{2,1,0:T(8,128)}) fusion(bf16[16,192,256]{2,1,0:T(8,128)(2,1)} %param.8), kind=kLoop, calls=%fused_computation.103 | loop fusion | bytes 12533760 | tf_op jit(solution)/shard_map/slice | solution.py:34
  14.3 5.8 %fusion.18 = f32[16,192,256]{2,1,0:T(8,128)S(1)} fusion(bf16[16,192,256]{2,1,0:T(8,128)(2,1)S(1)} %copy-done, f32[1,192,256]{2,1,0:T(8,128)S(1)} %collective-permute-done.1, f32[16,192,256]{2,1,0:T(8,128)} %convert_element_type.59, f32[1,192,256]{2,1,0:T(8,128)S(1)} %collective-permute-done, f32[16,192,255]{2,1,0:T(8,128)} %get-tuple-element.97, ...), kind=kLoop, calls=%fused_computation.28 | loop fusion | flops 18087936 | bytes 14558720 | tf_op jit(solution)/shard_map/sub | solution.py:37
  22.1 3.6 %collective-permute-start.3 = (f32[1,192,256]{2,1,0:T(8,128)S(1)}, f32[1,192,256]{2,1,0:T(8,128)S(1)}, u32[]{:S(2)}, u32[]{:S(2)}) collective-permute-start(f32[1,192,256]{2,1,0:T(8,128)S(1)} %get-tuple-element.95), channel_id=1, source_target_pairs={{1,0},{2,1},{3,2},{4,3},{5,4},{6,5},{7,6},{8,7},{9,8},{10,9},{11,1... | collective-permute-start | bytes 589832 | tf_op jit(solution)/shard_map/ppermute | solution.py:22
  28.9 3.9 %fusion.27 = bf16[16,192,256]{2,1,0:T(8,128)(2,1)} fusion(f32[16,192,256]{2,1,0:T(8,128)S(1)} %fusion.18, f32[1,192,256]{2,1,0:T(8,128)S(1)} %collective-permute-done.3, f32[1,192,256]{2,1,0:T(8,128)S(1)} %collective-permute-done.2, f32[16,192,255]{2,1,0:T(8,128)S(1)} %get-tuple-element.93, f32[16,192,255]{2,1,0:T(8,128)S(1)} %get-tuple-element.92, ...), kind=kLoop, calls=%fused_computation.38 | loop fusion | flops 18087936 | bytes 11412992 | tf_op jit(solution)/shard_map/convert_element_type | solution.py:93
  32.8 7.2 %all-to-all-start = ((bf16[16,192,256]{2,1,0:T(8,128)(2,1)}), bf16[16,192,256]{2,1,0:T(8,128)(2,1)}, u32[]{:S(2)}, u32[]{:S(2)}) async-start(bf16[16,192,256]{2,1,0:T(8,128)(2,1)} %fusion.27), calls=%async_computation | async-start | bytes 3145728 | tf_op jit(solution)/shard_map/all_to_all | solution.py:95
  40.9 27.2 %all-to-all-done = bf16[16,192,256]{2,1,0:T(8,128)(2,1)} async-done(((bf16[16,192,256]{2,1,0:T(8,128)(2,1)}), bf16[16,192,256]{2,1,0:T(8,128)(2,1)}, u32[]{:S(2)}, u32[]{:S(2)}) %all-to-all-start) | async-done | bytes 1572896 | tf_op jit(solution)/shard_map/all_to_all | solution.py:95
  68.0 117.2 %while.11 = (s32[]{:T(128)}, f32[6,1,512,256]{3,2,1,0:T(8,128)}, s32[6,8]{1,0:T(8,128)S(1)}, s32[48,24]{1,0:T(8,128)S(1)}, bf16[48,64,64]{2,1,0:T(8,128)(2,1)}, ...) while((s32[]{:T(128)}, f32[6,1,512,256]{3,2,1,0:T(8,128)}, ...), condition=%wide.region_1.2_spmd.clone, body=%wide.region_0.1_spmd.clone.sunk | while | flops 882388544 | bytes 19416056 | solution.py:65
  71.6 5.3 %convert_bitcast_fusion.2 = bf16[8,64,48,64]{3,2,1,0:T(8,128)(2,1)} fusion(bf16[8,24,64,64]{3,2,1,0:T(8,128)(2,1)S(1)} %bitcast.124, s32[8,24]{1,0:T(8,128)S(1)} %gather_fusion.2), kind=kOutput, calls=%fused_computation.4.clone.1 | convolution fusion | flops 77079552 | bytes 4719360 | tf_op jit(solution)/shard_map/while/body/eval_jaxpr/rjc,rjab->racb/dot_general | solution.py:57
  76.9 7.5 %reshape.228 = bf16[512,3072]{1,0:T(8,128)(2,1)S(1)} reshape(bf16[8,64,48,64]{3,2,1,0:T(8,128)(2,1)} %convert_bitcast_fusion.2) | data formatting | bytes 6291456 | tf_op jit(solution)/shard_map/while/body/eval_jaxpr/reshape | solution.py:58
  91.1 5.3 %convert_bitcast_fusion.2 = bf16[8,64,48,64]{3,2,1,0:T(8,128)(2,1)} fusion(bf16[8,24,64,64]{3,2,1,0:T(8,128)(2,1)S(1)} %bitcast.124, s32[8,24]{1,0:T(8,128)S(1)} %gather_fusion.2), kind=kOutput, calls=%fused_computation.4.clone.1 | convolution fusion | flops 77079552 | bytes 4719360 | tf_op jit(solution)/shard_map/while/body/eval_jaxpr/rjc,rjab->racb/dot_general | solution.py:57
  96.4 7.5 %reshape.228 = bf16[512,3072]{1,0:T(8,128)(2,1)S(1)} reshape(bf16[8,64,48,64]{3,2,1,0:T(8,128)(2,1)} %convert_bitcast_fusion.2) | data formatting | bytes 6291456 | tf_op jit(solution)/shard_map/while/body/eval_jaxpr/reshape | solution.py:58
  110.6 5.3 %convert_bitcast_fusion.2 = bf16[8,64,48,64]{3,2,1,0:T(8,128)(2,1)} fusion(bf16[8,24,64,64]{3,2,1,0:T(8,128)(2,1)S(1)} %bitcast.124, s32[8,24]{1,0:T(8,128)S(1)} %gather_fusion.2), kind=kOutput, calls=%fused_computation.4.clone.1 | convolution fusion | flops 77079552 | bytes 4719360 | tf_op jit(solution)/shard_map/while/body/eval_jaxpr/rjc,rjab->racb/dot_general | solution.py:57
  115.9 7.5 %reshape.228 = bf16[512,3072]{1,0:T(8,128)(2,1)S(1)} reshape(bf16[8,64,48,64]{3,2,1,0:T(8,128)(2,1)} %convert_bitcast_fusion.2) | data formatting | bytes 6291456 | tf_op jit(solution)/shard_map/while/body/eval_jaxpr/reshape | solution.py:58
  130.2 5.3 %convert_bitcast_fusion.2 = bf16[8,64,48,64]{3,2,1,0:T(8,128)(2,1)} fusion(bf16[8,24,64,64]{3,2,1,0:T(8,128)(2,1)S(1)} %bitcast.124, s32[8,24]{1,0:T(8,128)S(1)} %gather_fusion.2), kind=kOutput, calls=%fused_computation.4.clone.1 | convolution fusion | flops 77079552 | bytes 4719360 | tf_op jit(solution)/shard_map/while/body/eval_jaxpr/rjc,rjab->racb/dot_general | solution.py:57
  135.4 7.5 %reshape.228 = bf16[512,3072]{1,0:T(8,128)(2,1)S(1)} reshape(bf16[8,64,48,64]{3,2,1,0:T(8,128)(2,1)} %convert_bitcast_fusion.2) | data formatting | bytes 6291456 | tf_op jit(solution)/shard_map/while/body/eval_jaxpr/reshape | solution.py:58
  143.0 3.2 %fusion.71 = f32[6,1,512,256]{3,2,1,0:T(8,128)} fusion(f32[6,1,512,256]{3,2,1,0:T(8,128)} %get-tuple-element.154, s32[]{:T(128)} %get-tuple-element.153, bf16[512,3072]{1,0:T(8,128)(2,1)S(1)} %reshape.228, bf16[1,3072,256]{2,1,0:T(8,128)(2,1)} %get-tuple-element.167), kind=kOutput, calls=%fused_computation.9.clone.1 | convolution fusion | flops 805306368 | bytes 5243392 | tf_op jit(solution)/shard_map/while/body/eval_jaxpr/ak,rkl->ral/dot_general | solution.py:59
  149.7 5.3 %convert_bitcast_fusion.2 = bf16[8,64,48,64]{3,2,1,0:T(8,128)(2,1)} fusion(bf16[8,24,64,64]{3,2,1,0:T(8,128)(2,1)S(1)} %bitcast.124, s32[8,24]{1,0:T(8,128)S(1)} %gather_fusion.2), kind=kOutput, calls=%fused_computation.4.clone.1 | convolution fusion | flops 77079552 | bytes 4719360 | tf_op jit(solution)/shard_map/while/body/eval_jaxpr/rjc,rjab->racb/dot_general | solution.py:57
  155.0 7.5 %reshape.228 = bf16[512,3072]{1,0:T(8,128)(2,1)S(1)} reshape(bf16[8,64,48,64]{3,2,1,0:T(8,128)(2,1)} %convert_bitcast_fusion.2) | data formatting | bytes 6291456 | tf_op jit(solution)/shard_map/while/body/eval_jaxpr/reshape | solution.py:58
  162.5 3.2 %fusion.71 = f32[6,1,512,256]{3,2,1,0:T(8,128)} fusion(f32[6,1,512,256]{3,2,1,0:T(8,128)} %get-tuple-element.154, s32[]{:T(128)} %get-tuple-element.153, bf16[512,3072]{1,0:T(8,128)(2,1)S(1)} %reshape.228, bf16[1,3072,256]{2,1,0:T(8,128)(2,1)} %get-tuple-element.167), kind=kOutput, calls=%fused_computation.9.clone.1 | convolution fusion | flops 805306368 | bytes 5243392 | tf_op jit(solution)/shard_map/while/body/eval_jaxpr/ak,rkl->ral/dot_general | solution.py:59
  169.3 5.3 %convert_bitcast_fusion.2 = bf16[8,64,48,64]{3,2,1,0:T(8,128)(2,1)} fusion(bf16[8,24,64,64]{3,2,1,0:T(8,128)(2,1)S(1)} %bitcast.124, s32[8,24]{1,0:T(8,128)S(1)} %gather_fusion.2), kind=kOutput, calls=%fused_computation.4.clone.1 | convolution fusion | flops 77079552 | bytes 4719360 | tf_op jit(solution)/shard_map/while/body/eval_jaxpr/rjc,rjab->racb/dot_general | solution.py:57
  174.6 7.5 %reshape.228 = bf16[512,3072]{1,0:T(8,128)(2,1)S(1)} reshape(bf16[8,64,48,64]{3,2,1,0:T(8,128)(2,1)} %convert_bitcast_fusion.2) | data formatting | bytes 6291456 | tf_op jit(solution)/shard_map/while/body/eval_jaxpr/reshape | solution.py:58
  182.1 3.2 %fusion.71 = f32[6,1,512,256]{3,2,1,0:T(8,128)} fusion(f32[6,1,512,256]{3,2,1,0:T(8,128)} %get-tuple-element.154, s32[]{:T(128)} %get-tuple-element.153, bf16[512,3072]{1,0:T(8,128)(2,1)S(1)} %reshape.228, bf16[1,3072,256]{2,1,0:T(8,128)(2,1)} %get-tuple-element.167), kind=kOutput, calls=%fused_computation.9.clone.1 | convolution fusion | flops 805306368 | bytes 5243392 | tf_op jit(solution)/shard_map/while/body/eval_jaxpr/ak,rkl->ral/dot_general | solution.py:59
  188.4 26.0 %all_to_all.17 = bf16[16,1,192,256]{3,2,1,0:T(8,128)(2,1)S(1)} all-to-all(bf16[16,1,192,256]{3,2,1,0:T(8,128)(2,1)S(1)} %fusion.35), channel_id=1, replica_groups=mesh['spec'=16,'tile'=32] {'spec'}, dimensions={0} | all-to-all | bytes 3145728 | tf_op jit(solution)/shard_map/all_to_all | solution.py:99
  (93 shorter events, 45.6 us)
Async XLA Ops:
  1.0 13.3 %collective-permute-start = (f32[1,192,256]{2,1,0:T(8,128)S(1)}, f32[1,192,256]{2,1,0:T(8,128)S(1)}, u32[]{:S(2)}, u32[]{:S(2)}) collective-permute-start(f32[1,192,256]{2,1,0:T(8,128)S(1)} %get-tuple-element.98), channel_id=1, source_target_pairs={{0,1},{1,2},{2,3},{3,4},{4,5},{5,6},{6,7},{7,8},{8,9},{9,10},{10,1... | collective-permute-start | bytes 589832 | tf_op jit(solution)/shard_map/ppermute | solution.py:20
  2.9 9.3 %copy-start = (bf16[16,192,256]{2,1,0:T(8,128)(2,1)S(1)}, bf16[16,192,256]{2,1,0:T(8,128)(2,1)}, u32[]{:S(2)}) copy-start(bf16[16,192,256]{2,1,0:T(8,128)(2,1)} %param.8) | copy-start | bytes 4718596
  2.9 11.3 %collective-permute-start.1 = (f32[1,192,256]{2,1,0:T(8,128)S(1)}, f32[1,192,256]{2,1,0:T(8,128)S(1)}, u32[]{:S(2)}, u32[]{:S(2)}) collective-permute-start(f32[1,192,256]{2,1,0:T(8,128)S(1)} %get-tuple-element.99), channel_id=1, source_target_pairs={{1,0},{2,1},{3,2},{4,3},{5,4},{6,5},{7,6},{8,7},{9,8},{10,9},{11,1... | collective-permute-start | bytes 589832 | tf_op jit(solution)/shard_map/ppermute | solution.py:22
  12.2 2.1 copy-start.1
  12.2 2.1 copy-start.2
  20.2 7.0 %collective-permute-start.2 = (f32[1,192,256]{2,1,0:T(8,128)S(1)}, f32[1,192,256]{2,1,0:T(8,128)S(1)}, u32[]{:S(2)}, u32[]{:S(2)}) collective-permute-start(f32[1,192,256]{2,1,0:T(8,128)S(1)} %get-tuple-element.94), channel_id=1, source_target_pairs={{0,1},{1,2},{2,3},{3,4},{4,5},{5,6},{6,7},{7,8},{8,9},{9,10},{10,1... | collective-permute-start | bytes 589832 | tf_op jit(solution)/shard_map/ppermute | solution.py:20
  22.1 6.8 %collective-permute-start.3 = (f32[1,192,256]{2,1,0:T(8,128)S(1)}, f32[1,192,256]{2,1,0:T(8,128)S(1)}, u32[]{:S(2)}, u32[]{:S(2)}) collective-permute-start(f32[1,192,256]{2,1,0:T(8,128)S(1)} %get-tuple-element.95), channel_id=1, source_target_pairs={{1,0},{2,1},{3,2},{4,3},{5,4},{6,5},{7,6},{8,7},{9,8},{10,9},{11,1... | collective-permute-start | bytes 589832 | tf_op jit(solution)/shard_map/ppermute | solution.py:22
  32.8 7.2 %copy-start.3 = (s32[48,24]{0,1:T(8,128)S(1)}, s32[48,24]{0,1:T(8,128)}, u32[]{:S(2)}) copy-start(s32[48,24]{0,1:T(8,128)} %param.12) | copy-start | bytes 13828
  32.8 35.2 %all-to-all-start = ((bf16[16,192,256]{2,1,0:T(8,128)(2,1)}), bf16[16,192,256]{2,1,0:T(8,128)(2,1)}, u32[]{:S(2)}, u32[]{:S(2)}) async-start(bf16[16,192,256]{2,1,0:T(8,128)(2,1)} %fusion.27), calls=%async_computation | async-start | bytes 3145728 | tf_op jit(solution)/shard_map/all_to_all | solution.py:95
